TPU v7x, 32 devices: a whole 2x2x4 slice. The times are simulated.
32 devices in a mesh: row: 8 (over y, x, core), col: 4 (over z).
Axes of the slice: x: 2, y: 2, z: 4, core: 2. Of those that a mesh axis runs over, the one named last changes fastest.
Arguments:
- matrix: float32 [16384, 16384], P('row', 'col'), may hold values from -80 to 80
Outputs:
- reduced: float32 [16384, 16384], P('row', 'col')
All inputs are finite; a program needn't handle non-finite values.
Results may differ from a plain program's by a relative error of at most 0.0003.
Values sent between devices are 32-bit elements; how exact they have to be, the bound alone decides.
A program may use at most 128 MiB of HBM per device.

v0:
```python
import jax
import jax.numpy as jnp
from jax import lax
from jax.sharding import PartitionSpec as P

B = 64


highest = lax.Precision.HIGHEST


def from_root(x, axis, root):
    mine = lax.axis_index(axis) == root
    return lax.psum(jnp.where(mine, x, jnp.zeros_like(x)), axis)


def product(left, right):
    return jnp.dot(left, right, precision=highest, preferred_element_type=jnp.float32)


def cholesky_lower(gram_matrix):
    count = gram_matrix.shape[0]
    positions = jnp.arange(count, dtype=jnp.int32)

    def column_step(column, lower_factor):
        pick = jnp.where(positions == column, jnp.float32(1.0), jnp.float32(0.0))
        row_values = product(pick[None, :], lower_factor)[0]
        target = product(gram_matrix, pick[:, None])[:, 0]
        residual = target - product(lower_factor, row_values[:, None])[:, 0]
        pivot = jnp.sum(residual * pick)
        scaled = residual / jnp.sqrt(pivot)
        fresh = jnp.where(positions >= column, scaled, jnp.float32(0.0))
        return jnp.where(positions[None, :] == column, fresh[:, None], lower_factor)

    return lax.fori_loop(0, count, column_step, jnp.zeros_like(gram_matrix))


def invert_lower(lower_factor):
    count = lower_factor.shape[0]
    positions = jnp.arange(count, dtype=jnp.int32)
    identity = jnp.eye(count, dtype=jnp.float32)

    def row_step(index, inverse):
        pick = jnp.where(positions == index, jnp.float32(1.0), jnp.float32(0.0))
        row_values = product(pick[None, :], lower_factor)[0]
        pivot = jnp.sum(row_values * pick)
        target = product(pick[None, :], identity)[0]
        fresh = (target - product(row_values[None, :], inverse)[0]) / pivot
        return jnp.where(positions[:, None] == index, fresh[None, :], inverse)

    return lax.fori_loop(0, count, row_step, jnp.zeros_like(lower_factor))


def sign_lu(block):
    work = block
    count = block.shape[0]
    unit_lower = jnp.eye(count, dtype=block.dtype)
    signs = []
    for column in range(count):
        pivot = work[column, column]
        sign_value = jnp.where(pivot >= 0, -jnp.ones_like(pivot), jnp.ones_like(pivot))
        work = work.at[column, column].add(-sign_value)
        below = work[column + 1 :, column] / work[column, column]
        unit_lower = unit_lower.at[column + 1 :, column].set(below)
        work = work.at[column + 1 :, column + 1 :].add(
            -below[:, None] * work[column, column + 1 :][None, :]
        )
        signs.append(sign_value)
    return (unit_lower, jnp.triu(work), jnp.stack(signs))


def reconstruct(top_basis):
    unit_lower, upper, signs = sign_lu(top_basis)
    inverse_upper = invert_lower(upper.T).T
    inverse_lower = invert_lower(unit_lower)
    factor = -product(upper * signs[None, :], inverse_lower.T)
    return (inverse_upper, factor, signs)


def shards(matrix):
    height, breadth = matrix.shape
    col_index = lax.axis_index("col")
    row_start = lax.axis_index("row") * height
    col_start = col_index * breadth
    global_rows = row_start + jnp.arange(height, dtype=jnp.int32)
    global_cols = col_start + jnp.arange(breadth, dtype=jnp.int32)
    slots = jnp.arange(B, dtype=jnp.int32)
    current = matrix
    limit = B
    column_piece = from_root(current[:, 0:limit], "col", 0)
    panel_rows = jnp.where(global_rows[:, None] >= limit, column_piece, jnp.float32(0.0))
    row_piece = from_root(current[0:limit, :], "row", 0)
    panel_cols = jnp.where(global_cols[None, :] >= limit, row_piece, jnp.float32(0.0))
    onehot_rows = jnp.where(
        global_rows[:, None] - limit == slots[None, :], jnp.float32(1.0), jnp.float32(0.0)
    )
    onehot_cols = jnp.where(
        global_cols[:, None] - limit == slots[None, :], jnp.float32(1.0), jnp.float32(0.0)
    )
    gram_matrix, top_panel = lax.psum(
        (product(panel_rows.T, panel_rows), product(onehot_rows.T, panel_rows)), "row"
    )
    lower_factor = cholesky_lower(gram_matrix)
    lower_inverse = invert_lower(lower_factor)
    basis_rows = product(panel_rows, lower_inverse.T)
    basis_cols = product(lower_inverse, panel_cols)
    top_basis = product(top_panel, lower_inverse.T)
    inverse_upper, factor, signs = reconstruct(top_basis)
    shifted = signs[:, None] * inverse_upper
    vectors_rows = product(basis_rows, inverse_upper) - product(onehot_rows, shifted)
    vectors_cols = product(inverse_upper.T, basis_cols) - product(shifted.T, onehot_cols.T)
    image_rows = lax.psum(product(current, vectors_cols.T), "col")
    projected = lax.psum(product(vectors_rows.T, image_rows), "row")
    inner = product(factor.T, product(projected, factor))
    update_rows = product(image_rows, factor) - 0.5 * product(vectors_rows, inner)
    image_cols = lax.psum(product(vectors_rows.T, current), "row")
    update_cols = product(factor.T, image_cols) - 0.5 * product(inner.T, vectors_cols)
    current = current - product(vectors_rows, update_cols) - product(update_rows, vectors_cols)
    return current


def solution(mesh):
    placed = (P("row", "col"),)
    return jax.shard_map(
        shards, mesh=mesh, in_specs=placed, out_specs=P("row", "col"), check_vma=False
    )
```

profile of v0, /device:TPU:0, one launch (start us, length us, event | category | flops | bytes accessed | tf_op | source)
XLA Modules:
  0.0 992.4 jit_solution(12067611578896561898)
XLA Ops:
  6.5 2.3 slice_select_fusion.1
  8.9 2.3 slice_select_fusion
  11.2 53.2 %all-reduce.6.cloned.1.call-done = f32[2048,64]{1,0:T(8,128)} async-done(((f32[2048,64]{1,0:T(8,128)}), f32[2048,64]{1,0:T(8,128)}) %all-reduce.6.cloned.1.call-update) | async-done | bytes 524304 | tf_op jit(solution)/shard_map/psum | solution.py:14
  64.4 4.1 fusion.90
  68.5 3.0 fusion.80
  71.5 24.6 %all-reduce = (f32[64,64]{1,0:T(8,128)S(1)}, f32[64,64]{1,0:T(8,128)S(1)}) all-reduce(f32[64,64]{1,0:T(8,128)S(1)} %fusion.90, f32[64,64]{1,0:T(8,128)S(1)} %fusion.80), channel_id=1, replica_groups=mesh['row'=8,'col'=4] {'row'}, use_global_device_ids=true, to_apply=%region_1.2 | all-reduce | flops 8192 | bytes 65536 | tf_op jit(solution)/shard_map/psum | solution.py:100
  96.1 121.2 %while.250 = (s32[]{:T(128)}, f32[64,64]{1,0:T(8,128)S(1)}, f32[64,64]{1,0:T(8,128)S(1)}, s32[]{:T(128)}, s32[]{:T(128)}) while((s32[]{:T(128)}, f32[64,64]{1,0:T(8,128)S(1)}, f32[64,64]{1,0:T(8,128)S(1)}, s32[]{:T(128)}, s32[]{:T(128)}) %tuple.954), condition=%wide.region_4.5_spmd.clone.clone, body=%wide.region_2.4_spmd.clone.clone.sunk | while | flops 164674 | bytes 84213 | solution.py:35
  217.2 113.5 %while.247 = (s32[]{:T(128)}, f32[64,64]{1,0:T(8,128)S(1)}, f32[64,64]{1,0:T(8,128)S(1)}, s32[]{:T(128)}, s32[]{:T(128)}) while((s32[]{:T(128)}, f32[64,64]{1,0:T(8,128)S(1)}, f32[64,64]{1,0:T(8,128)S(1)}, s32[]{:T(128)}, s32[]{:T(128)}) %tuple.957), condition=%wide.region_7.8_spmd.clone, body=%wide.region_5.7_spmd.clone.sunk | while | flops 168642 | bytes 67300 | solution.py:51
  333.1 1.0 scatter-add.425
  336.9 0.9 scatter-add.429
  340.1 0.9 scatter-add.431
  343.3 0.9 scatter-add.435
  346.5 0.9 scatter-add.439
  349.7 0.9 scatter-add.441
  352.8 0.9 scatter-add.445
  356.0 0.9 scatter-add.449
  359.2 0.9 scatter-add.451
  362.6 0.9 scatter-add.455
  365.8 0.9 scatter-add.459
  368.9 0.9 scatter-add.461
  372.1 0.9 scatter-add.465
  375.3 0.9 scatter-add.469
  378.5 0.9 scatter-add.471
  523.3 104.8 %while.248 = (s32[]{:T(128)}, f32[64,64]{1,0:T(8,128)S(1)}, f32[64,64]{1,0:T(8,128)S(1)}, s32[]{:T(128)}, s32[]{:T(128)}) while((s32[]{:T(128)}, f32[64,64]{1,0:T(8,128)S(1)}, f32[64,64]{1,0:T(8,128)S(1)}, s32[]{:T(128)}, s32[]{:T(128)}) %tuple.960), condition=%wide.region_11.12_spmd.clone, body=%wide.region_9.11_spmd.clone.sunk | while | flops 168642 | bytes 67300 | solution.py:51
  628.1 2.3 fusion.88
  630.3 1.3 fusion.133
  631.8 1.4 convolution_subtract_fusion.1
  633.2 25.0 %fusion.134 = f32[64,4096]{1,0:T(8,128)} fusion(f32[2048,64]{0,1:T(8,128)S(1)} %convolution_subtract_fusion.1, f32[2048,4096]{1,0:T(8,128)} %param.389), kind=kOutput, calls=%fused_computation.419 | convolution fusion | flops 6442450944 | bytes 35127296 | tf_op jit(solution)/shard_map/dot_general | solution.py:18
  685.8 32.1 %all-reduce.10.cloned.1.call-done = (f32[64,4096]{1,0:T(8,128)}, f32[64,4096]{1,0:T(8,128)}) async-done(((f32[64,4096]{1,0:T(8,128)}, f32[64,4096]{1,0:T(8,128)}), (f32[64,4096]{1,0:T(8,128)}, f32[64,4096]{1,0:T(8,128)})) %all-reduce.10.cloned.1.call-update) | async-done | bytes 2097168 | tf_op jit(solution)/shard_map/psum | solution.py:116
  718.0 2.2 fusion.85
  720.2 1.0 fusion.136
  721.2 2.6 convolution_subtract_fusion
  723.8 36.3 %convolution_bitcast_fusion.9 = f32[2048,64]{0,1:T(8,128)} fusion(f32[64,4096]{1,0:T(8,128)S(1)} %convolution_subtract_fusion, f32[2048,4096]{1,0:T(8,128)} %param.389), kind=kOutput, calls=%fused_computation.105 | convolution fusion | flops 6442450944 | bytes 35127296 | tf_op jit(solution)/shard_map/dot_general | solution.py:18
  760.2 121.6 %while.249 = (s32[]{:T(128)}, f32[64,64]{1,0:T(8,128)S(1)}, f32[64,64]{1,0:T(8,128)S(1)}, s32[]{:T(128)}, s32[]{:T(128)}) while((s32[]{:T(128)}, f32[64,64]{1,0:T(8,128)S(1)}, f32[64,64]{1,0:T(8,128)S(1)}, s32[]{:T(128)}, s32[]{:T(128)}) %tuple.963), condition=%wide.region_14.15_spmd.clone, body=%wide.region_12.14_spmd.clone.sunk | while | flops 168642 | bytes 67300 | solution.py:51
  762.2 0.8 fusion.223
  764.1 0.8 fusion.223
  767.9 0.8 fusion.223
  769.8 0.8 fusion.223
  771.7 0.8 fusion.223
  775.5 0.8 fusion.223
  882.0 2.3 fusion.135
  884.3 1.7 fusion.137
  886.0 22.6 %psum.55 = f32[64,64]{1,0:T(8,128)S(1)} all-reduce(f32[64,64]{1,0:T(8,128)S(1)} %fusion.137), channel_id=1, replica_groups=mesh['row'=8,'col'=4] {'row'}, use_global_device_ids=true, to_apply=%region_18.19 | all-reduce | flops 4096 | bytes 32768 | tf_op jit(solution)/shard_map/psum | solution.py:113
  909.0 1.0 fusion.76
  910.1 30.3 %fusion.140 = f32[2048,4096]{1,0:T(8,128)} fusion(f32[2048,64]{0,1:T(8,128)S(1)} %convolution_subtract_fusion.1, f32[64,4096]{1,0:T(8,128)S(1)} %fusion.76), kind=kOutput, calls=%fused_computation.425 | convolution fusion | flops 6442450944 | bytes 35127296 | tf_op jit(solution)/shard_map/dot_general | solution.py:18
  940.4 1.8 fusion.141
  942.2 1.8 fusion.77
  944.0 41.3 %subtract_subtract_fusion = f32[2048,4096]{1,0:T(8,128)} fusion(f32[2048,4096]{1,0:T(8,128)} %param.389, f32[2048,4096]{1,0:T(8,128)} %fusion.140, f32[2048,64]{1,0:T(8,128)S(1)} %fusion.77, f32[64,4096]{1,0:T(8,128)S(1)} %convolution_subtract_fusion), kind=kOutput, calls=%fused_computation.98 | convolution fusion | flops 6459228160 | bytes 102236160 | tf_op jit(solution)/shard_map/dot_general | solution.py:18
  (1789 shorter events, 531.3 us)
Async XLA Ops:
  6.5 57.8 %all-reduce.6.cloned.1.call-start = ((), (), s32[]{:S(2)}) async-start(), calls=%async_computation | async-start | bytes 2097152 | tf_op jit(solution)/shard_map/psum | solution.py:14
  8.8 709.1 %all-reduce.10.cloned.1.call-start = ((), (), s32[]{:S(2)}) async-start(), calls=%async_computation.2 | async-start | bytes 4194304 | tf_op jit(solution)/shard_map/psum | solution.py:116
  658.2 226.1 %all-reduce.8.cloned.1.call-start = ((), (), s32[]{:S(2)}) async-start(), calls=%async_computation.1 | async-start | bytes 1048576 | tf_op jit(solution)/shard_map/psum | solution.py:112
  884.3 56.1 %copy-start = (f32[2048,64]{0,1:T(8,128)S(1)}, f32[2048,64]{0,1:T(8,128)}, u32[]{:S(2)}) copy-start(f32[2048,64]{0,1:T(8,128)} %all-reduce.8.cloned.1.call-done) | copy-start | bytes 1572868
Sparse Core Ops, SparseCore 0:
  9.7 54.6 all-reduce.5
  658.3 59.5 all-reduce.9
  760.3 37.9 all-reduce.7
where the time goes:
time: 1010 us; the launch traced here: 992 us
  matrix products  552 us (55%)
  local copies, waits for them, and re-layouts  118 us (12%)
  between operations  99.1 us (10%)
  waiting for transfers between devices  85.3 us (8%)
  loops' own time  47.3 us (5%)
  blocking collectives  47.2 us (5%)
  other arithmetic  42.5 us (4%)
    dot_general x789, matrix products, product(): jnp.dot(left, right, precision=highest, preferred_element_type=jnp.float32)  552 us
    psum x1, waiting for transfers between devices, from_root(): return lax.psum(jnp.where(mine, x, jnp.zeros_like(x)), axis)  53.2 us
    another operation x1, loops' own time, cholesky_lower(): return lax.fori_loop(0, count, column_step, jnp.zeros_like(gram_matrix))  45.4 us
    scatter-add x63, local copies, waits for them, and re-layouts, sign_lu(): work.at[column + 1:, column + 1:]  43.5 us
    another operation x63, local copies, waits for them, and re-layouts  32.8 us
    psum x1, waiting for transfers between devices, shards(): image_cols = lax.psum(product(vectors_rows.T, current), 'row')  32.1 us
    scatter x63, local copies, waits for them, and re-layouts, sign_lu(): unit_lower = unit_lower.at[column + 1:, column].set(below)  26.7 us
    psum x1, blocking collectives, shards(): lax.psum((product(panel_rows.T, panel_rows), product(onehot_rows.T, panel...  24.6 us
  transfers between devices with their start and end apart: 3, of which 2 were waited for; matrix products, arithmetic and copies ran while one was open for 15% of the time, Pallas kernels for 0%

commit v1 on v0

v1 whole, which is shorter than its diff:
```python
import jax
import jax.numpy as jnp
from jax import lax
from jax.experimental import pallas as pl
from jax.experimental.pallas import tpu as pltpu
from jax.sharding import PartitionSpec as P

B = 64


highest = lax.Precision.HIGHEST
high = lax.Precision.HIGH
f32 = jnp.float32


def from_root(x, axis, root):
    mine = lax.axis_index(axis) == root
    return lax.psum(jnp.where(mine, x, jnp.zeros_like(x)), axis)


def product(left, right, precision=highest):
    return jnp.dot(left, right, precision=precision, preferred_element_type=f32)


def product_nt(left, right):
    return lax.dot_general(
        left, right, (((1,), (1,)), ((), ())), precision=highest, preferred_element_type=f32
    )


def factor_values(gram, top):
    rows = lax.broadcasted_iota(jnp.int32, (B, 2 * B), 0)
    lanes = lax.broadcasted_iota(jnp.int32, (B, 2 * B), 1)
    eye = jnp.where(rows + B == lanes, f32(1.0), f32(0.0))
    small_rows = lax.broadcasted_iota(jnp.int32, (B, B), 0)
    small_lanes = lax.broadcasted_iota(jnp.int32, (B, B), 1)
    eye_half = jnp.where(small_rows == small_lanes, f32(1.0), f32(0.0))
    work = jnp.concatenate([gram, eye_half], axis=1)
    for j in range(B):
        inverse = 1.0 / jnp.sqrt(work[j : j + 1, j : j + 1])
        row = work[j : j + 1, :] * inverse
        column = work[:, j : j + 1] * inverse
        lowered = work - column * row
        work = jnp.where(rows > j, lowered, jnp.where(rows == j, row, work))
    lower_inverse = work[:, B:]
    top_basis = product_nt(top, lower_inverse)
    top_turned = product_nt(lower_inverse, top)
    q = jnp.concatenate([top_basis, eye_half], axis=1)
    t = jnp.concatenate([top_turned, eye_half], axis=1)
    signs = jnp.zeros((1, B), f32)
    sign_lane = lax.broadcasted_iota(jnp.int32, (1, B), 1)
    reciprocals = jnp.zeros((B, 1), f32)
    sublane = lax.broadcasted_iota(jnp.int32, (B, 1), 0)
    one_row = lax.broadcasted_iota(jnp.int32, (1, 2 * B), 1)
    for j in range(B):
        pivot = q[j : j + 1, j : j + 1]
        sign = jnp.where(pivot >= 0, f32(-1.0), f32(1.0))
        inverse = 1.0 / (pivot - sign)
        row_q = q[j : j + 1, :] - jnp.where(one_row == j, sign, f32(0.0))
        row_t = t[j : j + 1, :] - jnp.where(one_row == j, sign, f32(0.0))
        below_q = q[:, j : j + 1] * inverse
        below_t = t[:, j : j + 1] * inverse
        q = jnp.where(rows > j, q - below_q * row_q, jnp.where(rows == j, row_q, q))
        t = jnp.where(rows > j, t - below_t * row_t, t)
        signs = jnp.where(sign_lane == j, sign, signs)
        reciprocals = jnp.where(sublane == j, inverse, reciprocals)
    upper = jnp.where(small_lanes >= small_rows, q[:, :B], f32(0.0))
    unit_inverse = q[:, B:]
    upper_inverse_turned = t[:, B:] * reciprocals
    factor = -product_nt(upper * signs, unit_inverse)
    first = product(upper_inverse_turned, lower_inverse)
    second = upper_inverse_turned * signs
    return first, second, factor


def factor_kernel(gram_ref, top_ref, first_ref, second_ref, factor_ref):
    first, second, factor = factor_values(gram_ref[...], top_ref[...])
    first_ref[...] = first
    second_ref[...] = second
    factor_ref[...] = factor


def factors(gram, top):
    vmem = pl.BlockSpec(memory_space=pltpu.VMEM)
    return pl.pallas_call(
        factor_kernel,
        out_shape=[jax.ShapeDtypeStruct((B, B), f32)] * 3,
        in_specs=[vmem] * 2,
        out_specs=[vmem] * 3,
    )(gram, top)


def shards(matrix):
    height, breadth = matrix.shape
    col_index = lax.axis_index("col")
    row_start = lax.axis_index("row") * height
    col_start = col_index * breadth
    global_rows = row_start + jnp.arange(height, dtype=jnp.int32)
    global_cols = col_start + jnp.arange(breadth, dtype=jnp.int32)
    slots = jnp.arange(B, dtype=jnp.int32)
    current = matrix
    limit = B
    column_piece = from_root(current[:, 0:limit], "col", 0)
    panel_rows = jnp.where(global_rows[:, None] >= limit, column_piece, jnp.float32(0.0))
    row_piece = from_root(current[0:limit, :], "row", 0)
    panel_cols = jnp.where(global_cols[None, :] >= limit, row_piece, jnp.float32(0.0))
    onehot_rows = jnp.where(
        global_rows[:, None] - limit == slots[None, :], jnp.float32(1.0), jnp.float32(0.0)
    )
    onehot_cols = jnp.where(
        global_cols[:, None] - limit == slots[None, :], jnp.float32(1.0), jnp.float32(0.0)
    )
    gram_matrix, top_panel = lax.psum(
        (product(panel_rows.T, panel_rows), product(onehot_rows.T, panel_rows)), "row"
    )
    first, second, factor = factors(gram_matrix, top_panel)
    vectors_rows = product(panel_rows, first.T) - product(onehot_rows, second.T)
    vectors_cols = product(first, panel_cols) - product(second, onehot_cols.T)
    image_rows = lax.psum(product(current, vectors_cols.T, high), "col")
    projected = lax.psum(product(vectors_rows.T, image_rows), "row")
    inner = product(factor.T, product(projected, factor))
    update_rows = product(image_rows, factor) - 0.5 * product(vectors_rows, inner)
    image_cols = lax.psum(product(vectors_rows.T, current, high), "row")
    update_cols = product(factor.T, image_cols) - 0.5 * product(inner.T, vectors_cols)
    current = current - product(
        jnp.concatenate([vectors_rows, update_rows], 1), jnp.concatenate([update_cols, vectors_cols], 0), high
    )
    return current


def solution(mesh):
    placed = (P("row", "col"),)
    return jax.shard_map(
        shards, mesh=mesh, in_specs=placed, out_specs=P("row", "col"), check_vma=False
    )
```

time: 1010 us -> 320 us (0.32); the launches traced: 992 us -> 320 us
  matrix products: 552 us -> 91.4 us
  local copies, waits for them, and re-layouts: 118 us -> 0.01 us
  between operations: 99.1 us -> 13.2 us
  waiting for transfers between devices: 85.3 us -> 148 us
  loops' own time: 47.3 us -> 0 us
  other arithmetic: 42.5 us -> 4.57 us
  Pallas kernels: 0 us -> 14.1 us
    dot_general x789 -> x16, matrix products: 552 us -> 91.4 us  [product(): return jnp.dot(left, right, precision=precision, preferred_element_type=f32)]
    psum x1 -> x2, waiting for transfers between devices: 53.2 us -> 112 us  [from_root(): return lax.psum(jnp.where(mine, x, jnp.zeros_like(x)), axis)]
    scatter-add x127 -> x0, local copies, waits for them, and re-layouts: 53.5 us -> none  [the longest x63 43.5 us: sign_lu(): work.at[column + 1:, column + 1:]]
    another operation x4 -> x0, loops' own time: 47.3 us -> none  [the longest x1 45.4 us: cholesky_lower(): return lax.fori_loop(0, count, column_step, jnp.zeros_like(gram_matrix))]
    another operation x64 -> x0, local copies, waits for them, and re-layouts: 32.9 us -> none
    scatter x63 -> x0, local copies, waits for them, and re-layouts: 26.7 us -> none  [sign_lu(): unit_lower = unit_lower.at[column + 1:, column].set(below)]
    select_n x320 -> x0, other arithmetic: 19.8 us -> none  [the longest x192 14.7 us: row_step(): return jnp.where(positions[:, None] == index, fresh[None, :], inverse)]
    pallas_call x0 -> x1, Pallas kernels: none -> 14.1 us  [factors(): pl.pallas_call(factor_kernel, out_shape=[jax.ShapeDtypeStruct((B, B), f32...]
  transfers between devices with their start and end apart: 3 -> 3, of which waited for: 2 -> 3; matrix products, arithmetic and copies ran while one was open for 15% -> 1% of each run, Pallas kernels for 0% -> 0%
where the time goes in v1:
time: 320 us
  waiting for transfers between devices  148 us (46%)
  matrix products  91.4 us (29%)
  blocking collectives  48.3 us (15%)
  Pallas kernels  14.1 us (4%)
  between operations  13.2 us (4%)
  other arithmetic  4.57 us (1%)
    psum x2, waiting for transfers between devices, from_root(): return lax.psum(jnp.where(mine, x, jnp.zeros_like(x)), axis)  112 us
    dot_general x16, matrix products, product(): return jnp.dot(left, right, precision=precision, preferred_element_type=f32)  91.4 us
    psum x1, waiting for transfers between devices, shards(): image_rows = lax.psum(product(current, vectors_cols.T, high), 'col')  35.6 us
    psum x1, blocking collectives, shards(): lax.psum((product(panel_rows.T, panel_rows), product(onehot_rows.T, panel...  25.1 us
    psum x1, blocking collectives, shards(): projected = lax.psum(product(vectors_rows.T, image_rows), 'row')  23.1 us
    pallas_call x1, Pallas kernels, factors(): pl.pallas_call(factor_kernel, out_shape=[jax.ShapeDtypeStruct((B, B), f32...  14.1 us
  transfers between devices with their start and end apart: 3, of which 3 were waited for; matrix products, arithmetic and copies ran while one was open for 1% of the time, Pallas kernels for 0%

profile of v1, /device:TPU:0, one launch (start us, length us, event | category | flops | bytes accessed | tf_op | source)
XLA Modules:
  0.0 319.8 jit_solution(8518128045562123912)
XLA Ops:
  6.5 0.0 all-reduce.6.cloned.1.call-start
  6.5 2.3 slice_select_fusion.1
  8.8 0.0 all-reduce.6.cloned.1.call-update
  8.8 0.0 all-reduce.10.cloned.1.call-start
  8.9 2.3 slice_select_fusion
  11.2 53.2 %all-reduce.6.cloned.1.call-done = f32[2048,64]{1,0:T(8,128)} async-done(((f32[2048,64]{1,0:T(8,128)}), f32[2048,64]{1,0:T(8,128)}) %all-reduce.6.cloned.1.call-update) | async-done | bytes 524304 | tf_op jit(solution)/shard_map/psum | solution.py:18
  64.4 4.1 %fusion.20 = f32[64,64]{1,0:T(8,128)S(1)} fusion(f32[2048,64]{1,0:T(8,128)} %all-reduce.6.cloned.1.call-done, pred[2048]{0:T(1024)(128)(4,1)S(1)} %fusion.38), kind=kOutput, calls=%fused_computation.30 | convolution fusion | flops 100794368 | bytes 542720 | tf_op jit(solution)/shard_map/dot_general | solution.py:22
  68.5 3.0 fusion.7
  71.5 25.1 %all-reduce = (f32[64,64]{1,0:T(8,128)}, f32[64,64]{1,0:T(8,128)}) all-reduce(f32[64,64]{1,0:T(8,128)S(1)} %fusion.20, f32[64,64]{1,0:T(8,128)S(1)} %fusion.7), channel_id=1, replica_groups=mesh['row'=8,'col'=4] {'row'}, use_global_device_ids=true, to_apply=%region_1.2 | all-reduce | flops 8192 | bytes 65536 | tf_op jit(solution)/shard_map/psum | solution.py:113
  96.6 14.1 %shard_map.17 = (f32[64,64]{1,0:T(8,128)}, f32[64,64]{1,0:T(8,128)}, f32[64,64]{1,0:T(8,128)}) custom-call(f32[64,64]{1,0:T(8,128)} %get-tuple-element.11.gram_ref, f32[64,64]{1,0:T(8,128)} %get-tuple-element.12.top_ref), custom_call_target="tpu_custom_call" | custom-call | tf_op jit(solution)/shard_map/pallas_call | solution.py:85
  110.7 0.0 copy-start.2
  110.7 0.0 copy-start.1
  110.7 2.7 fusion.17
  113.4 2.2 convolution_subtract_fusion.2
  115.6 0.0 copy-start
  115.6 17.5 %fusion.53 = f32[64,4096]{1,0:T(8,128)} fusion(f32[2048,64]{0,1:T(8,128)S(1)} %convolution_subtract_fusion.2, f32[2048,4096]{1,0:T(8,128)} %param.1), kind=kOutput, calls=%fused_computation.65 | convolution fusion | flops 3221225472 | bytes 35127296 | tf_op jit(solution)/shard_map/dot_general | solution.py:22
  133.0 0.0 all-reduce.10.cloned.1.call-update
  133.1 0.3 all-reduce.8.cloned.1.call-start
  133.4 59.1 %all-reduce.10.cloned.1.call-done = (f32[64,4096]{1,0:T(8,128)}, f32[64,4096]{1,0:T(8,128)}) async-done(((f32[64,4096]{1,0:T(8,128)}, f32[64,4096]{1,0:T(8,128)}), (f32[64,4096]{1,0:T(8,128)}, f32[64,4096]{1,0:T(8,128)})) %all-reduce.10.cloned.1.call-update) | async-done | bytes 2097168 | tf_op jit(solution)/shard_map/psum | solution.py:18
  192.5 0.0 copy-done.2
  192.5 2.2 fusion.15
  194.7 0.0 copy-done.1
  194.7 3.2 %convolution_subtract_fusion.1 = f32[64,4096]{1,0:T(8,128)S(1)} fusion(f32[64,4096]{1,0:T(8,128)S(1)} %fusion.15, f32[64,64]{1,0:T(8,128)S(1)} %copy-done.1, s32[4096]{0:T(1024)S(1)} %fusion.35), kind=kOutput, calls=%fused_computation.3 | convolution fusion | flops 202113024 | bytes 2129920 | tf_op jit(solution)/shard_map/dot_general | solution.py:22
  198.0 22.0 %convolution_bitcast_fusion = f32[2048,64]{0,1:T(8,128)} fusion(f32[64,4096]{1,0:T(8,128)S(1)} %convolution_subtract_fusion.1, f32[2048,4096]{1,0:T(8,128)} %param.1), kind=kOutput, calls=%fused_computation.7 | convolution fusion | flops 3221225472 | bytes 35127296 | tf_op jit(solution)/shard_map/dot_general | solution.py:22
  220.0 0.0 all-reduce.8.cloned.1.call-update
  220.0 0.0 copy-done
  220.0 2.2 fusion.54
  222.3 35.6 %all-reduce.8.cloned.1.call-done = f32[2048,64]{0,1:T(8,128)} async-done(((f32[2048,64]{0,1:T(8,128)}), f32[2048,64]{0,1:T(8,128)}) %all-reduce.8.cloned.1.call-update) | async-done | bytes 524304 | tf_op jit(solution)/shard_map/psum | solution.py:119
  257.9 1.6 fusion.50
  259.5 23.1 %psum.54 = f32[64,64]{1,0:T(8,128)S(1)} all-reduce(f32[64,64]{1,0:T(8,128)S(1)} %fusion.50), channel_id=1, replica_groups=mesh['row'=8,'col'=4] {'row'}, use_global_device_ids=true, to_apply=%region_5.6 | all-reduce | flops 4096 | bytes 32768 | tf_op jit(solution)/shard_map/psum | solution.py:120
  282.7 0.2 fusion.51
  282.8 0.2 fusion.52
  283.1 1.1 fusion
  284.1 1.7 fusion.49
  285.8 0.6 fusion.1
  286.4 26.9 %convolution_subtract_fusion = f32[2048,4096]{1,0:T(8,128)} fusion(f32[2048,4096]{1,0:T(8,128)} %param.1, f32[64,4096]{1,0:T(8,128)S(1)} %convolution_subtract_fusion.1, f32[64,4096]{1,0:T(8,128)S(1)} %fusion, f32[2048,64]{0,1:T(8,128)S(1)} %fusion.1, f32[2048,64]{0,1:T(8,128)S(1)} %convolution_subtract_fusion.2), kind=kOutput, calls=%fused_computation | convolution fusion | flops 6451625984 | bytes 70254592 | tf_op jit(solution)/shard_map/dot_general | solution.py:22
  (4 shorter events, 0.0 us)
Async XLA Ops:
  6.5 57.8 %all-reduce.6.cloned.1.call-start = ((), (), s32[]{:S(2)}) async-start(), calls=%async_computation | async-start | bytes 2097152 | tf_op jit(solution)/shard_map/psum | solution.py:18
  8.8 183.7 %all-reduce.10.cloned.1.call-start = ((), (), s32[]{:S(2)}) async-start(), calls=%async_computation.2 | async-start | bytes 4194304 | tf_op jit(solution)/shard_map/psum | solution.py:18
  110.7 81.8 %copy-start.2 = (f32[64,64]{1,0:T(8,128)S(1)}, f32[64,64]{1,0:T(8,128)}, u32[]{:S(2)}) copy-start(f32[64,64]{1,0:T(8,128)} %get-tuple-element.8) | copy-start | bytes 49156
  110.7 84.0 %copy-start.1 = (f32[64,64]{1,0:T(8,128)S(1)}, f32[64,64]{1,0:T(8,128)}, u32[]{:S(2)}) copy-start(f32[64,64]{1,0:T(8,128)} %get-tuple-element.9) | copy-start | bytes 49156
  115.6 104.5 %copy-start = (f32[64,64]{1,0:T(8,128)S(1)}, f32[64,64]{1,0:T(8,128)}, u32[]{:S(2)}) copy-start(f32[64,64]{1,0:T(8,128)} %get-tuple-element.10) | copy-start | bytes 49156
  133.1 124.8 %all-reduce.8.cloned.1.call-start = ((), (), s32[]{:S(2)}) async-start(), calls=%async_computation.1 | async-start | bytes 1048576 | tf_op jit(solution)/shard_map/psum | solution.py:119
Sparse Core Ops, SparseCore 0:
  9.7 54.6 all-reduce.5
  133.2 59.2 all-reduce.9
  220.2 37.6 all-reduce.7

commit v2 on v1

v2 whole, which is shorter than its diff:
```python
import jax
import jax.numpy as jnp
from jax import lax
from jax.experimental import pallas as pl
from jax.experimental.pallas import tpu as pltpu
from jax.sharding import PartitionSpec as P

B = 64


highest = lax.Precision.HIGHEST
MESH = pl.DeviceIdType.MESH
high = lax.Precision.HIGH
f32 = jnp.float32


def product(left, right, precision=highest):
    return jnp.dot(left, right, precision=precision, preferred_element_type=f32)


def product_nt(left, right):
    return lax.dot_general(
        left, right, (((1,), (1,)), ((), ())), precision=highest, preferred_element_type=f32
    )


def factor_values(gram, top):
    rows = lax.broadcasted_iota(jnp.int32, (B, 2 * B), 0)
    lanes = lax.broadcasted_iota(jnp.int32, (B, 2 * B), 1)
    eye = jnp.where(rows + B == lanes, f32(1.0), f32(0.0))
    small_rows = lax.broadcasted_iota(jnp.int32, (B, B), 0)
    small_lanes = lax.broadcasted_iota(jnp.int32, (B, B), 1)
    eye_half = jnp.where(small_rows == small_lanes, f32(1.0), f32(0.0))
    work = jnp.concatenate([gram, eye_half], axis=1)
    for j in range(B):
        inverse = 1.0 / jnp.sqrt(work[j : j + 1, j : j + 1])
        row = work[j : j + 1, :] * inverse
        column = work[:, j : j + 1] * inverse
        lowered = work - column * row
        work = jnp.where(rows > j, lowered, jnp.where(rows == j, row, work))
    lower_inverse = work[:, B:]
    top_basis = product_nt(top, lower_inverse)
    top_turned = product_nt(lower_inverse, top)
    q = jnp.concatenate([top_basis, eye_half], axis=1)
    t = jnp.concatenate([top_turned, eye_half], axis=1)
    signs = jnp.zeros((1, B), f32)
    sign_lane = lax.broadcasted_iota(jnp.int32, (1, B), 1)
    reciprocals = jnp.zeros((B, 1), f32)
    sublane = lax.broadcasted_iota(jnp.int32, (B, 1), 0)
    one_row = lax.broadcasted_iota(jnp.int32, (1, 2 * B), 1)
    for j in range(B):
        pivot = q[j : j + 1, j : j + 1]
        sign = jnp.where(pivot >= 0, f32(-1.0), f32(1.0))
        inverse = 1.0 / (pivot - sign)
        row_q = q[j : j + 1, :] - jnp.where(one_row == j, sign, f32(0.0))
        row_t = t[j : j + 1, :] - jnp.where(one_row == j, sign, f32(0.0))
        below_q = q[:, j : j + 1] * inverse
        below_t = t[:, j : j + 1] * inverse
        q = jnp.where(rows > j, q - below_q * row_q, jnp.where(rows == j, row_q, q))
        t = jnp.where(rows > j, t - below_t * row_t, t)
        signs = jnp.where(sign_lane == j, sign, signs)
        reciprocals = jnp.where(sublane == j, inverse, reciprocals)
    upper = jnp.where(small_lanes >= small_rows, q[:, :B], f32(0.0))
    unit_inverse = q[:, B:]
    upper_inverse_turned = t[:, B:] * reciprocals
    factor = -product_nt(upper * signs, unit_inverse)
    factor_turned = -product_nt(unit_inverse, upper * signs)
    first = product(upper_inverse_turned, lower_inverse)
    second = upper_inverse_turned * signs
    return first, second, factor, factor_turned


def remote(src, dst, send_sem, recv_sem, device):
    return pltpu.make_async_remote_copy(
        src_ref=src,
        dst_ref=dst,
        send_sem=send_sem,
        recv_sem=recv_sem,
        device_id=device,
        device_id_type=MESH,
    )


def greet_all(height, breadth, me_row, me_col):
    count = height * breadth
    me = me_row * breadth + me_col
    barrier = pltpu.get_barrier_semaphore()

    def signal(step, carry):
        other = lax.rem(me + step, count)
        pl.semaphore_signal(
            barrier,
            inc=1,
            device_id=(other // breadth, lax.rem(other, breadth)),
            device_id_type=MESH,
        )
        return carry

    lax.fori_loop(1, count, signal, 0)
    pl.semaphore_wait(barrier, count - 1)


def gather_axis(buffer, mine, count, target, send_sems, recv_sems, skip=None):
    for step in range(1, count):
        other = lax.rem(mine + step, count)
        copy = remote(
            buffer.at[mine], buffer.at[mine], send_sems.at[step], recv_sems.at[mine], target(other)
        )
        if skip is None:
            copy.start()
        else:
            pl.when(other != skip)(copy.start)


def gather_sent(buffer, mine, count, target, send_sems, recv_sems, skip=None):
    for step in range(1, count):
        other = lax.rem(mine + step, count)
        copy = remote(
            buffer.at[mine], buffer.at[mine], send_sems.at[step], recv_sems.at[mine], target(other)
        )
        if skip is None:
            copy.wait_send()
        else:
            pl.when(other != skip)(copy.wait_send)


def gather_received(buffer, mine, count, target, send_sems, recv_sems):
    for step in range(1, count):
        other = lax.rem(mine + step, count)
        remote(
            buffer.at[other], buffer.at[other], send_sems.at[step], recv_sems.at[other], target(other)
        ).wait_recv()


def spread_kernel(
    height, breadth, own, pc, pr, stats, ex,
    local_sem, scatter_sems, role_sems, role_local, plane_sems, pc_sems, line_sems, pr_sems,
    ex_sends, ex_recvs,
):
    me_row, me_col = lax.axis_index("row"), lax.axis_index("col")
    width = own.shape[2]
    next_row = lax.rem(me_row + 1, height)
    in_plane = lambda other: (other, me_col)
    in_line = lambda other: (me_row, other)
    root = me_row == 0
    chunk = me_row * breadth + me_col
    local_role = jnp.logical_and(root, chunk // height == me_col)

    greet_all(height, breadth, me_row, me_col)

    def scatter_copy(i):
        return remote(own.at[i], pc.at[i], scatter_sems.at[i], pc_sems.at[i], (i, me_col))

    def role_copy(i):
        g = me_col * height + i
        k = lax.rem(g, breadth)
        r = g // breadth
        itself = jnp.logical_and(r == 0, k == me_col)
        return itself, remote(own.at[i], pr.at[k], role_sems.at[i], pr_sems.at[k], (r, k)), k

    def first_copy(j):
        return remote(own.at[0], pc.at[0], plane_sems.at[j], pc_sems.at[0], (j, me_col))

    @pl.when(root)
    def _():
        for i in range(1, height):
            scatter_copy(i).start()
        for i in range(height):
            itself, copy, k = role_copy(i)
            pl.when(jnp.logical_not(itself))(copy.start)
            local = pltpu.make_async_copy(own.at[i], pr.at[k], role_local)
            pl.when(itself)(local.start)
        for j in range(1, height):
            first_copy(j).start()
        whole = pltpu.make_async_copy(own, pc, local_sem)
        whole.start()
        whole.wait()

    @pl.when(local_role)
    def _():
        pltpu.make_async_copy(own.at[0], pr.at[me_col], role_local).wait()

    @pl.when(jnp.logical_not(root))
    def _():
        remote(
            pc.at[me_row], pc.at[me_row], plane_sems.at[0], pc_sems.at[me_row], (next_row, me_col)
        ).wait_recv()
        gather_axis(pc, me_row, height, in_plane, plane_sems, pc_sems, skip=0)

    @pl.when(jnp.logical_not(local_role))
    def _():
        remote(
            pr.at[me_col], pr.at[me_col], line_sems.at[0], pr_sems.at[me_col], (next_row, me_col)
        ).wait_recv()

    gather_axis(pr, me_col, breadth, in_line, line_sems, pr_sems)

    @pl.when(jnp.logical_not(root))
    def _():
        gather_received(pc, me_row, height, in_plane, plane_sems, pc_sems)

    gram = jnp.zeros((B, B), f32)
    top = jnp.zeros((B, B), f32)
    positions = lax.broadcasted_iota(jnp.int32, (width, B), 0)
    slots = lax.broadcasted_iota(jnp.int32, (width, B), 1)
    for i in range(height):
        piece = pc[i]
        start = (me_col * height + i) * width - B
        gram = gram + product_nt(piece, piece)
        onehot = jnp.where(positions + start == slots, f32(1.0), f32(0.0))
        top = top + product(piece, onehot)
    ex[me_col] = jnp.concatenate([gram, top], axis=1)
    gather_axis(ex, me_col, breadth, in_line, ex_sends, ex_recvs)
    gather_received(ex, me_col, breadth, in_line, ex_sends, ex_recvs)
    total = ex[0]
    for k in range(1, breadth):
        total = total + ex[k]
    stats[...] = total
    gather_received(pr, me_col, breadth, in_line, line_sems, pr_sems)
    gather_sent(ex, me_col, breadth, in_line, ex_sends, ex_recvs)
    gather_sent(pr, me_col, breadth, in_line, line_sems, pr_sems)

    @pl.when(root)
    def _():
        for i in range(1, height):
            scatter_copy(i).wait_send()
        for i in range(height):
            itself, copy, _ = role_copy(i)
            pl.when(jnp.logical_not(itself))(copy.wait_send)
        for j in range(1, height):
            first_copy(j).wait_send()

    @pl.when(jnp.logical_not(root))
    def _():
        gather_sent(pc, me_row, height, in_plane, plane_sems, pc_sems, skip=0)


def spread(own, height, breadth):
    width = own.shape[2]
    vmem = pl.BlockSpec(memory_space=pltpu.VMEM)
    dma = pltpu.SemaphoreType.DMA
    return pl.pallas_call(
        lambda *refs: spread_kernel(height, breadth, *refs),
        out_shape=[
            jax.ShapeDtypeStruct((height, B, width), f32),
            jax.ShapeDtypeStruct((breadth, B, width), f32),
            jax.ShapeDtypeStruct((B, 2 * B), f32),
        ],
        in_specs=[vmem],
        out_specs=[vmem] * 3,
        scratch_shapes=[
            pltpu.VMEM((breadth, B, 2 * B), f32),
            dma(()),
            dma((height,)),
            dma((height,)),
            dma(()),
            dma((height,)),
            dma((height,)),
            dma((breadth,)),
            dma((breadth,)),
            dma((breadth,)),
            dma((breadth,)),
        ],
        compiler_params=pltpu.CompilerParams(collective_id=0, has_side_effects=True),
        name="spread",
    )(own)


def vectors_kernel(height, breadth, stats, pc, pr, vc, vr, factor_ref, turned_ref):
    first, second, factor, turned = factor_values(stats[:, :B], stats[:, B:].T)
    factor_ref[...] = factor
    turned_ref[...] = turned
    width = pc.shape[2]
    slots = lax.broadcasted_iota(jnp.int32, (B, width), 0)
    positions = lax.broadcasted_iota(jnp.int32, (B, width), 1)
    for pieces, out, base, count in (
        (pc, vc, lax.axis_index("col") * height, height),
        (pr, vr, lax.axis_index("row") * breadth, breadth),
    ):
        for i in range(count):
            start = (base + i) * width - B
            onehot = jnp.where(positions + start == slots, f32(1.0), f32(0.0))
            out[:, i * width : (i + 1) * width] = product(first, pieces[i]) - product(
                second, onehot
            )


def vectors_of(stats, pc, pr, height, breadth):
    width = pc.shape[2]
    vmem = pl.BlockSpec(memory_space=pltpu.VMEM)
    return pl.pallas_call(
        lambda *refs: vectors_kernel(height, breadth, *refs),
        out_shape=[
            jax.ShapeDtypeStruct((B, height * width), f32),
            jax.ShapeDtypeStruct((B, breadth * width), f32),
            jax.ShapeDtypeStruct((B, B), f32),
            jax.ShapeDtypeStruct((B, B), f32),
        ],
        in_specs=[vmem] * 3,
        out_specs=[vmem] * 4,
        name="vectors",
    )(stats, pc, pr)


def image_kernel(
    height, breadth, z, vc, wc, wr, projected, rs, ex,
    rs_sends, rs_recvs, line_sems, wr_sems, role_sem, plane_sems, wc_sems, ex_sends, ex_recvs,
):
    me_row, me_col = lax.axis_index("row"), lax.axis_index("col")
    width = z.shape[2]
    in_plane = lambda other: (other, me_col)
    in_line = lambda other: (me_row, other)
    chunk = me_row * breadth + me_col
    to_row = lax.rem(chunk, height)
    to_col = chunk // height
    itself = jnp.logical_and(to_row == me_row, to_col == me_col)

    greet_all(height, breadth, me_row, me_col)

    def part_copy(step):
        other = lax.rem(me_col + step, breadth)
        return remote(
            z.at[other], rs.at[me_col], rs_sends.at[step], rs_recvs.at[me_col], in_line(other)
        )

    for step in range(1, breadth):
        part_copy(step).start()
    rs[me_col] = z[me_col]
    gather_received(rs, me_col, breadth, in_line, rs_sends, rs_recvs)
    total = rs[0]
    for k in range(1, breadth):
        total = total + rs[k]
    wr[me_col] = total
    role = remote(wr.at[me_col], wc.at[to_row], role_sem, wc_sems.at[to_row], (to_row, to_col))

    @pl.when(jnp.logical_not(itself))
    def _():
        role.start()

    gather_axis(wr, me_col, breadth, in_line, line_sems, wr_sems)

    @pl.when(itself)
    def _():
        wc[me_row] = total

    @pl.when(jnp.logical_not(itself))
    def _():
        remote(
            wc.at[me_row], wc.at[me_row], plane_sems.at[0], wc_sems.at[me_row],
            (lax.rem(me_row + 1, height), me_col),
        ).wait_recv()

    gather_axis(wc, me_row, height, in_plane, plane_sems, wc_sems)
    gather_received(wc, me_row, height, in_plane, plane_sems, wc_sems)
    partial = jnp.zeros((B, B), f32)
    for i in range(height):
        partial = partial + product_nt(wc[i], vc[:, i * width : (i + 1) * width])
    ex[me_col] = jnp.concatenate([partial, jnp.zeros((B, B), f32)], axis=1)
    gather_axis(ex, me_col, breadth, in_line, ex_sends, ex_recvs)
    gather_received(ex, me_col, breadth, in_line, ex_sends, ex_recvs)
    summed = ex[0]
    for k in range(1, breadth):
        summed = summed + ex[k]
    projected[...] = summed
    gather_received(wr, me_col, breadth, in_line, line_sems, wr_sems)
    for step in range(1, breadth):
        part_copy(step).wait_send()

    @pl.when(jnp.logical_not(itself))
    def _():
        role.wait_send()

    gather_sent(wr, me_col, breadth, in_line, line_sems, wr_sems)
    gather_sent(wc, me_row, height, in_plane, plane_sems, wc_sems)
    gather_sent(ex, me_col, breadth, in_line, ex_sends, ex_recvs)


def images(z, vc, height, breadth):
    width = z.shape[2]
    vmem = pl.BlockSpec(memory_space=pltpu.VMEM)
    dma = pltpu.SemaphoreType.DMA
    return pl.pallas_call(
        lambda *refs: image_kernel(height, breadth, *refs),
        out_shape=[
            jax.ShapeDtypeStruct((height, B, width), f32),
            jax.ShapeDtypeStruct((breadth, B, width), f32),
            jax.ShapeDtypeStruct((B, 2 * B), f32),
        ],
        in_specs=[vmem] * 2,
        out_specs=[vmem] * 3,
        scratch_shapes=[
            pltpu.VMEM((breadth, B, width), f32),
            pltpu.VMEM((breadth, B, 2 * B), f32),
            dma((breadth,)),
            dma((breadth,)),
            dma((breadth,)),
            dma((breadth,)),
            dma(()),
            dma((height,)),
            dma((height,)),
            dma((breadth,)),
            dma((breadth,)),
        ],
        compiler_params=pltpu.CompilerParams(collective_id=1, has_side_effects=True),
        name="images",
    )(z, vc)


def updates_kernel(height, breadth, projected, factor, turned, vc, vr, wc, wr, left, right):
    inner = product(turned[...], product(projected[:, :B], factor[...]))
    width = wc.shape[2]
    right[B:, :] = vc[...]
    left[:B, :] = vr[...]
    for i in range(height):
        part = slice(i * width, (i + 1) * width)
        right[:B, part] = product(turned[...], wc[i]) - 0.5 * product(inner, vc[:, part])
    for i in range(breadth):
        part = slice(i * width, (i + 1) * width)
        left[B:, part] = product(turned[...], wr[i]) - 0.5 * product(inner, vr[:, part])


def updates(projected, factor, turned, vc, vr, wc, wr):
    height, breadth = wc.shape[0], wr.shape[0]
    vmem = pl.BlockSpec(memory_space=pltpu.VMEM)
    return pl.pallas_call(
        lambda *refs: updates_kernel(height, breadth, *refs),
        out_shape=[
            jax.ShapeDtypeStruct((2 * B, vr.shape[1]), f32),
            jax.ShapeDtypeStruct((2 * B, vc.shape[1]), f32),
        ],
        in_specs=[vmem] * 7,
        out_specs=[vmem] * 2,
        name="updates",
    )(projected, factor, turned, vc, vr, wc, wr)


def shards(height, breadth, matrix):
    rows, cols = matrix.shape
    width = cols // height
    global_cols = lax.axis_index("col") * cols + jnp.arange(cols, dtype=jnp.int32)
    masked = jnp.where(global_cols[None, :] >= B, matrix[0:B, :], f32(0.0))
    own = masked.reshape(B, height, width).transpose(1, 0, 2)
    pc, pr, stats = spread(own, height, breadth)
    vc, vr, factor, turned = vectors_of(stats, pc, pr, height, breadth)
    image = lax.dot_general(
        vc, matrix, (((1,), (1,)), ((), ())), precision=high, preferred_element_type=f32
    )
    z = image.reshape(B, breadth, width).transpose(1, 0, 2)
    wc, wr, projected = images(z, vc, height, breadth)
    left, right = updates(projected, factor, turned, vc, vr, wc, wr)
    return matrix - lax.dot_general(
        left, right, (((0,), (0,)), ((), ())), precision=high, preferred_element_type=f32
    )


def solution(mesh):
    placed = (P("row", "col"),)
    height, breadth = mesh.shape["row"], mesh.shape["col"]
    return jax.shard_map(
        lambda matrix: shards(height, breadth, matrix),
        mesh=mesh,
        in_specs=placed,
        out_specs=P("row", "col"),
        check_vma=False,
    )
```

time: 320 us -> 166 us (0.52)
  waiting for transfers between devices: 148 us -> 0 us
  Pallas kernels: 14.1 us -> 111 us
  blocking collectives: 48.3 us -> 0 us
  matrix products: 91.4 us -> 51.8 us
  between operations: 13.2 us -> 0.03 us
  other arithmetic: 4.57 us -> 1.31 us
    psum x3 -> x0, waiting for transfers between devices: 148 us -> none  [the longest x2 112 us: from_root(): return lax.psum(jnp.where(mine, x, jnp.zeros_like(x)), axis)]
    pallas_call x1 -> x4, Pallas kernels: 14.1 us -> 111 us  [the longest x1 50.2 us: images(): pl.pallas_call(lambda *refs: image_kernel(height, breadth, *refs), out_sh...]
    psum x2 -> x0, blocking collectives: 48.3 us -> none  [the longest x1 25.1 us: shards(): lax.psum((product(panel_rows.T, panel_rows), product(onehot_rows.T, panel...]
    dot_general x16 -> x2, matrix products: 91.4 us -> 51.8 us  [the longest x1 30.4 us: shards(): lax.dot_general(left, right, (((0,), (0,)), ((), ())), precision=high, pr...]
    select_n x2 -> x1, other arithmetic: 4.54 us -> 1.3 us  [shards(): masked = jnp.where(global_cols[None, :] >= B, matrix[0:B, :], f32(0.0))]
  transfers between devices with their start and end apart: 3 -> 0, of which waited for: 3 -> 0; matrix products, arithmetic and copies ran while one was open for 1% -> 0% of each run, Pallas kernels for 0% -> 0%
where the time goes in v2:
time: 166 us
  Pallas kernels  111 us (67%)
  matrix products  51.8 us (31%)
  local copies, waits for them, and re-layouts  1.89 us (1%)
    pallas_call x1, Pallas kernels, images(): pl.pallas_call(lambda *refs: image_kernel(height, breadth, *refs), out_sh...  50.2 us
    pallas_call x1, Pallas kernels, spread(): pl.pallas_call(lambda *refs: spread_kernel(height, breadth, *refs), out_s...  36.6 us
    dot_general x1, matrix products, shards(): lax.dot_general(left, right, (((0,), (0,)), ((), ())), precision=high, pr...  30.4 us
    dot_general x1, matrix products, shards(): lax.dot_general(vc, matrix, (((1,), (1,)), ((), ())), precision=high, pre...  21.4 us
    pallas_call x1, Pallas kernels, vectors_of(): pl.pallas_call(lambda *refs: vectors_kernel(height, breadth, *refs), out_...  17.6 us
    pallas_call x1, Pallas kernels, updates(): pl.pallas_call(lambda *refs: updates_kernel(height, breadth, *refs), out_...  6.35 us

profile of v2, /device:TPU:0, one launch (start us, length us, event | category | flops | bytes accessed | tf_op | source)
XLA Modules:
  0.0 165.8 jit_solution(11745996704623752510)
XLA Ops:
  0.0 1.3 slice_select_fusion
  1.3 1.1 copy.8
  2.4 36.6 %spread.1 = (f32[8,64,512]{2,1,0:T(8,128)}, f32[4,64,512]{2,1,0:T(8,128)}, f32[64,128]{1,0:T(8,128)}) custom-call(f32[8,64,512]{2,1,0:T(8,128)} %bitcast.18), custom_call_target="tpu_custom_call" | custom-call | tf_op jit(solution)/shard_map/spread/pallas_call | solution.py:242
  39.0 17.6 %vectors.1 = (f32[64,4096]{1,0:T(8,128)}, f32[64,2048]{1,0:T(8,128)}, f32[64,64]{1,0:T(8,128)}, f32[64,64]{1,0:T(8,128)}) custom-call(f32[64,128]{1,0:T(8,128)} %get-tuple-element.17.refs_0_, f32[8,64,512]{2,1,0:T(8,128)} %get-tuple-element.18.refs_1_, f32[4,64,512]{2,1,0:T(8,128)} %get-tuple-element.19.refs_2_), custom_call_target="tpu_custom_call" | custom-call | tf_op jit(solution)/shard_map/vectors/pallas_call | solution.py:291
  56.6 21.4 %fusion = f32[64,2048]{1,0:T(8,128)S(1)} fusion(f32[64,4096]{1,0:T(8,128)} %get-tuple-element.20.refs_1_.refs_3_, f32[2048,4096]{1,0:T(8,128)} %param.1), kind=kOutput, calls=%fused_computation.5 | convolution fusion | flops 3221225472 | bytes 35127296 | tf_op jit(solution)/shard_map/dot_general | solution.py:445
  78.0 0.8 copy.9
  78.9 50.2 %images.1 = (f32[8,64,512]{2,1,0:T(8,128)}, f32[4,64,512]{2,1,0:T(8,128)}, f32[64,128]{1,0:T(8,128)}) custom-call(f32[4,64,512]{2,1,0:T(8,128)} %bitcast.21, f32[64,4096]{1,0:T(8,128)} %get-tuple-element.20.refs_1_.refs_3_), custom_call_target="tpu_custom_call" | custom-call | tf_op jit(solution)/shard_map/images/pallas_call | solution.py:382
  129.1 6.3 %updates.1 = (f32[128,2048]{1,0:T(8,128)}, f32[128,4096]{1,0:T(8,128)}) custom-call(f32[64,128]{1,0:T(8,128)} %get-tuple-element.21.refs_0_, f32[64,64]{1,0:T(8,128)} %get-tuple-element.22.refs_1_, f32[64,64]{1,0:T(8,128)} %get-tuple-element.23.refs_2_, f32[64,4096]{1,0:T(8,128)} %get-tuple-element.20.refs_1_.refs_3_, f32[64,2048]{1,0:T(8,128)} %get-tuple-element.24.refs_4_, ...), custom_call_target="tpu_custom_call" | custom-call | tf_op jit(solution)/shard_map/updates/pallas_call | solution.py:425
  135.4 30.4 %convolution_subtract_fusion = f32[2048,4096]{1,0:T(8,128)} fusion(f32[2048,4096]{1,0:T(8,128)} %param.1, f32[128,2048]{1,0:T(8,128)} %get-tuple-element.27, f32[128,4096]{1,0:T(8,128)} %get-tuple-element.28), kind=kOutput, calls=%fused_computation | convolution fusion | flops 6450839552 | bytes 70254592 | tf_op jit(solution)/shard_map/dot_general | solution.py:451
  (1 shorter events, 0.0 us)

commit v3 on v2

--- a/solution.py
+++ b/solution.py
@@ -10,12 +10,17 @@
 
 highest = lax.Precision.HIGHEST
 MESH = pl.DeviceIdType.MESH
-high = lax.Precision.HIGH
 f32 = jnp.float32
-
-
-def product(left, right, precision=highest):
-    return jnp.dot(left, right, precision=precision, preferred_element_type=f32)
+bf16 = jnp.bfloat16
+
+
+def product(left, right):
+    return jnp.dot(left, right, precision=highest, preferred_element_type=f32)
+
+
+def split(x):
+    upper = x.astype(bf16)
+    return upper, (x - upper.astype(f32)).astype(bf16)
 
 
 def product_nt(left, right):
@@ -266,7 +271,7 @@
     )(own)
 
 
-def vectors_kernel(height, breadth, stats, pc, pr, vc, vr, factor_ref, turned_ref):
+def vectors_kernel(height, breadth, stats, pc, pr, vc, vr, factor_ref, turned_ref, halves):
     first, second, factor, turned = factor_values(stats[:, :B], stats[:, B:].T)
     factor_ref[...] = factor
     turned_ref[...] = turned
@@ -283,6 +288,9 @@
             out[:, i * width : (i + 1) * width] = product(first, pieces[i]) - product(
                 second, onehot
             )
+    upper, lower = split(vc[...])
+    halves[:B, :] = upper
+    halves[B:, :] = lower
 
 
 def vectors_of(stats, pc, pr, height, breadth):
@@ -295,9 +303,10 @@
             jax.ShapeDtypeStruct((B, breadth * width), f32),
             jax.ShapeDtypeStruct((B, B), f32),
             jax.ShapeDtypeStruct((B, B), f32),
+            jax.ShapeDtypeStruct((2 * B, height * width), bf16),
         ],
         in_specs=[vmem] * 3,
-        out_specs=[vmem] * 4,
+        out_specs=[vmem] * 5,
         name="vectors",
     )(stats, pc, pr)
 
@@ -406,17 +415,84 @@
     )(z, vc)
 
 
+def image_part_kernel(block, halves, out):
+    nt = (((1,), (1,)), ((), ()))
+    rows, cols = block.shape
+    size = min(512, cols)
+    both = jnp.zeros((rows, 2 * B), f32)
+    for start in range(0, cols, size):
+        part = slice(start, start + size)
+        upper, lower = split(block[:, part])
+        both = both + lax.dot_general(upper, halves[:, part], nt, preferred_element_type=f32)
+        low = lax.dot_general(lower, halves[:, part], nt, preferred_element_type=f32)
+        both = both + jnp.where(lax.broadcasted_iota(jnp.int32, both.shape, 1) < B, low, f32(0.0))
+    turned = both.T
+    out[0] = turned[:B, :] + turned[B:, :]
+
+
+def image_part(matrix, halves, width):
+    rows, cols = matrix.shape
+    return pl.pallas_call(
+        image_part_kernel,
+        grid=(rows // width,),
+        out_shape=jax.ShapeDtypeStruct((rows // width, B, width), f32),
+        in_specs=[
+            pl.BlockSpec((width, cols), lambda i: (i, 0)),
+            pl.BlockSpec((2 * B, cols), lambda i: (0, 0)),
+        ],
+        out_specs=pl.BlockSpec((1, B, width), lambda i: (i, 0, 0)),
+        name="image_part",
+    )(matrix, halves)
+
+
+def final_kernel(block, left, right, out):
+    cols = block.shape[1]
+    size = min(512, cols)
+    for start in range(0, cols, size):
+        part = slice(start, start + size)
+        out[:, part] = block[:, part] - jnp.dot(
+            left[...], right[:, part], preferred_element_type=f32
+        )
+
+
+def final(matrix, left, right):
+    rows, cols = matrix.shape
+    tile = min(256, rows)
+    depth = left.shape[1]
+    return pl.pallas_call(
+        final_kernel,
+        grid=(rows // tile,),
+        out_shape=jax.ShapeDtypeStruct((rows, cols), f32),
+        in_specs=[
+            pl.BlockSpec((tile, cols), lambda i: (i, 0)),
+            pl.BlockSpec((tile, depth), lambda i: (i, 0)),
+            pl.BlockSpec((depth, cols), lambda i: (0, 0)),
+        ],
+        out_specs=pl.BlockSpec((tile, cols), lambda i: (i, 0)),
+        name="final",
+    )(matrix, left, right)
+
+
 def updates_kernel(height, breadth, projected, factor, turned, vc, vr, wc, wr, left, right):
     inner = product(turned[...], product(projected[:, :B], factor[...]))
+    mix = jnp.concatenate([turned[...], -0.5 * inner], axis=1)
     width = wc.shape[2]
-    right[B:, :] = vc[...]
-    left[:B, :] = vr[...]
     for i in range(height):
         part = slice(i * width, (i + 1) * width)
-        right[:B, part] = product(turned[...], wc[i]) - 0.5 * product(inner, vc[:, part])
+        v = vc[:, part]
+        u = product(mix, jnp.concatenate([wc[i], v], axis=0))
+        upper, lower = split(jnp.concatenate([u, v], axis=0))
+        right[: 2 * B, part] = upper
+        right[2 * B : 4 * B, part] = upper
+        right[4 * B :, part] = lower
     for i in range(breadth):
         part = slice(i * width, (i + 1) * width)
-        left[B:, part] = product(turned[...], wr[i]) - 0.5 * product(inner, vr[:, part])
+        v = vr[:, part]
+        u = product(mix, jnp.concatenate([wr[i], v], axis=0))
+        upper, lower = split(jnp.concatenate([v, u], axis=0).T)
+        left[part, : 2 * B] = upper
+        left[part, 2 * B : 4 * B] = lower
+        left[part, 4 * B :] = upper
 
 
 def updates(projected, factor, turned, vc, vr, wc, wr):
@@ -425,8 +501,8 @@
     return pl.pallas_call(
         lambda *refs: updates_kernel(height, breadth, *refs),
         out_shape=[
-            jax.ShapeDtypeStruct((2 * B, vr.shape[1]), f32),
-            jax.ShapeDtypeStruct((2 * B, vc.shape[1]), f32),
+            jax.ShapeDtypeStruct((vr.shape[1], 6 * B), bf16),
+            jax.ShapeDtypeStruct((6 * B, vc.shape[1]), bf16),
         ],
         in_specs=[vmem] * 7,
         out_specs=[vmem] * 2,
@@ -441,16 +517,11 @@
     masked = jnp.where(global_cols[None, :] >= B, matrix[0:B, :], f32(0.0))
     own = masked.reshape(B, height, width).transpose(1, 0, 2)
     pc, pr, stats = spread(own, height, breadth)
-    vc, vr, factor, turned = vectors_of(stats, pc, pr, height, breadth)
-    image = lax.dot_general(
-        vc, matrix, (((1,), (1,)), ((), ())), precision=high, preferred_element_type=f32
-    )
-    z = image.reshape(B, breadth, width).transpose(1, 0, 2)
+    vc, vr, factor, turned, halves = vectors_of(stats, pc, pr, height, breadth)
+    z = image_part(matrix, halves, width)
     wc, wr, projected = images(z, vc, height, breadth)
     left, right = updates(projected, factor, turned, vc, vr, wc, wr)
-    return matrix - lax.dot_general(
-        left, right, (((0,), (0,)), ((), ())), precision=high, preferred_element_type=f32
-    )
+    return final(matrix, left, right)
 
 
 def solution(mesh):

time: 166 us -> 155 us (0.934)
  matrix products: 51.8 us -> 0 us
  Pallas kernels: 111 us -> 152 us
    dot_general x2 -> x0, matrix products: 51.8 us -> none  [the longest x1 30.4 us: shards(): lax.dot_general(left, right, (((0,), (0,)), ((), ())), precision=high, pr...]
    pallas_call x0 -> x2, Pallas kernels: none -> 42.2 us  [the longest x1 27 us: final(): pl.pallas_call(final_kernel, grid=(rows // tile,), out_shape=jax.ShapeDty...]
where the time goes in v3:
time: 155 us
  Pallas kernels  152 us (98%)
    pallas_call x1, Pallas kernels, images(): pl.pallas_call(lambda *refs: image_kernel(height, breadth, *refs), out_sh...  50.2 us
    pallas_call x1, Pallas kernels, spread(): pl.pallas_call(lambda *refs: spread_kernel(height, breadth, *refs), out_s...  36.6 us
    pallas_call x1, Pallas kernels, final(): pl.pallas_call(final_kernel, grid=(rows // tile,), out_shape=jax.ShapeDty...  27 us
    pallas_call x1, Pallas kernels, vectors_of(): pl.pallas_call(lambda *refs: vectors_kernel(height, breadth, *refs), out_...  17.6 us
    pallas_call x1, Pallas kernels, image_part(): pl.pallas_call(image_part_kernel, grid=(rows // width,), out_shape=jax.Sh...  15.3 us
    pallas_call x1, Pallas kernels, updates(): pl.pallas_call(lambda *refs: updates_kernel(height, breadth, *refs), out_...  5.54 us

profile of v3, /device:TPU:0, one launch (start us, length us, event | category | flops | bytes accessed | tf_op | source)
XLA Modules:
  0.0 154.6 jit_solution(13467080516093853942)
XLA Ops:
  0.0 1.3 slice_select_fusion
  1.3 1.1 copy.5
  2.4 36.6 %spread.1 = (f32[8,64,512]{2,1,0:T(8,128)}, f32[4,64,512]{2,1,0:T(8,128)}, f32[64,128]{1,0:T(8,128)}) custom-call(f32[8,64,512]{2,1,0:T(8,128)} %bitcast.7), custom_call_target="tpu_custom_call" | custom-call | tf_op jit(solution)/shard_map/spread/pallas_call | solution.py:247
  39.0 17.6 %vectors.1 = (f32[64,4096]{1,0:T(8,128)}, f32[64,2048]{1,0:T(8,128)}, f32[64,64]{1,0:T(8,128)}, f32[64,64]{1,0:T(8,128)}, bf16[128,4096]{1,0:T(8,128)(2,1)}) custom-call(f32[64,128]{1,0:T(8,128)} %get-tuple-element.18.refs_0_, f32[8,64,512]{2,1,0:T(8,128)} %get-tuple-element.19.refs_1_, f32[4,64,512]{2,1,0:T(8,128)} %get-tuple-element.20.refs_2_), custom_call_target="tpu_custom_call" | custom-call | tf_op jit(solution)/shard_map/vectors/pallas_call | solution.py:299
  56.6 15.3 %image_part.1.refs_0_ = f32[4,64,512]{2,1,0:T(8,128)} custom-call(f32[2048,4096]{1,0:T(8,128)} %block.3, bf16[128,4096]{1,0:T(8,128)(2,1)} %get-tuple-element.21.halves), custom_call_target="tpu_custom_call" | custom-call | tf_op jit(solution)/shard_map/image_part/pallas_call | solution.py:435
  71.9 50.2 %images.1 = (f32[8,64,512]{2,1,0:T(8,128)}, f32[4,64,512]{2,1,0:T(8,128)}, f32[64,128]{1,0:T(8,128)}) custom-call(f32[4,64,512]{2,1,0:T(8,128)} %image_part.1.refs_0_, f32[64,4096]{1,0:T(8,128)} %get-tuple-element.22.refs_1_.refs_3_), custom_call_target="tpu_custom_call" | custom-call | tf_op jit(solution)/shard_map/images/pallas_call | solution.py:391
  122.1 5.5 %updates.1 = (bf16[2048,384]{1,0:T(8,128)(2,1)}, bf16[384,4096]{1,0:T(8,128)(2,1)}) custom-call(f32[64,128]{1,0:T(8,128)} %get-tuple-element.23.refs_0_, f32[64,64]{1,0:T(8,128)} %get-tuple-element.24.refs_1_, f32[64,64]{1,0:T(8,128)} %get-tuple-element.25.refs_2_, f32[64,4096]{1,0:T(8,128)} %get-tuple-element.22.refs_1_.refs_3_, ...), custom_call_target="tpu_custom_call" | custom-call | tf_op jit(solution)/shard_map/updates/pallas_call | solution.py:501
  127.7 27.0 %final.1 = f32[2048,4096]{1,0:T(8,128)} custom-call(f32[2048,4096]{1,0:T(8,128)} %block.3, bf16[2048,384]{1,0:T(8,128)(2,1)} %get-tuple-element.29.left, bf16[384,4096]{1,0:T(8,128)(2,1)} %get-tuple-element.30.right), custom_call_target="tpu_custom_call" | custom-call | tf_op jit(solution)/shard_map/final/pallas_call | solution.py:462
  (1 shorter events, 0.0 us)

commit v4 on v3

--- a/solution.py
+++ b/solution.py
@@ -137,6 +137,49 @@
         ).wait_recv()
 
 
+def pair_copies(buffer, mine, count, target, send_sems, recv_sems, skip):
+    partner = mine + 1 - 2 * lax.rem(mine, 2)
+
+    def copy(slot, step, other):
+        made = remote(
+            buffer.at[slot], buffer.at[slot], send_sems.at[step], recv_sems.at[slot], target(other)
+        )
+        return other != skip, made
+
+    direct = []
+    passed = []
+    for step in range(2, count, 2):
+        other = lax.rem(mine + step, count)
+        direct.append(copy(mine, step, other))
+        passed.append((other, copy(other, step + 1, partner)))
+    direct.append(copy(mine, 1, partner))
+    return partner, direct, passed
+
+
+def pair_gather(buffer, mine, count, target, send_sems, recv_sems, skip=-1):
+    partner, direct, passed = pair_copies(buffer, mine, count, target, send_sems, recv_sems, skip)
+
+    def received(slot):
+        remote(
+            buffer.at[slot], buffer.at[slot], send_sems.at[0], recv_sems.at[slot], target(partner)
+        ).wait_recv()
+
+    for allowed, copy in direct:
+        pl.when(allowed)(copy.start)
+    for slot, (allowed, copy) in passed:
+        received(slot)
+        pl.when(allowed)(copy.start)
+    received(partner)
+    for step in range(2, count, 2):
+        received(lax.rem(partner + step, count))
+
+
+def pair_sent(buffer, mine, count, target, send_sems, recv_sems, skip=-1):
+    _, direct, passed = pair_copies(buffer, mine, count, target, send_sems, recv_sems, skip)
+    for allowed, copy in direct + [entry for _, entry in passed]:
+        pl.when(allowed)(copy.wait_send)
+
+
 def spread_kernel(
     height, breadth, own, pc, pr, stats, ex,
     local_sem, scatter_sems, role_sems, role_local, plane_sems, pc_sems, line_sems, pr_sems,
@@ -163,8 +206,15 @@
         itself = jnp.logical_and(r == 0, k == me_col)
         return itself, remote(own.at[i], pr.at[k], role_sems.at[i], pr_sems.at[k], (r, k)), k
 
-    def first_copy(j):
-        return remote(own.at[0], pc.at[0], plane_sems.at[j], pc_sems.at[0], (j, me_col))
+    def first_copies():
+        made = [
+            remote(own.at[0], pc.at[0], plane_sems.at[j], pc_sems.at[0], (j, me_col))
+            for j in [1] + list(range(2, height, 2))
+        ]
+        return made + [
+            remote(own.at[m], pc.at[m], plane_sems.at[m + 1], pc_sems.at[m], (1, me_col))
+            for m in range(2, height, 2)
+        ]
 
     @pl.when(root)
     def _():
@@ -175,8 +225,8 @@
             pl.when(jnp.logical_not(itself))(copy.start)
             local = pltpu.make_async_copy(own.at[i], pr.at[k], role_local)
             pl.when(itself)(local.start)
-        for j in range(1, height):
-            first_copy(j).start()
+        for copy in first_copies():
+            copy.start()
         whole = pltpu.make_async_copy(own, pc, local_sem)
         whole.start()
         whole.wait()
@@ -190,7 +240,6 @@
         remote(
             pc.at[me_row], pc.at[me_row], plane_sems.at[0], pc_sems.at[me_row], (next_row, me_col)
         ).wait_recv()
-        gather_axis(pc, me_row, height, in_plane, plane_sems, pc_sems, skip=0)
 
     @pl.when(jnp.logical_not(local_role))
     def _():
@@ -202,7 +251,7 @@
 
     @pl.when(jnp.logical_not(root))
     def _():
-        gather_received(pc, me_row, height, in_plane, plane_sems, pc_sems)
+        pair_gather(pc, me_row, height, in_plane, plane_sems, pc_sems, skip=0)
 
     gram = jnp.zeros((B, B), f32)
     top = jnp.zeros((B, B), f32)
@@ -232,12 +281,12 @@
         for i in range(height):
             itself, copy, _ = role_copy(i)
             pl.when(jnp.logical_not(itself))(copy.wait_send)
-        for j in range(1, height):
-            first_copy(j).wait_send()
+        for copy in first_copies():
+            copy.wait_send()
 
     @pl.when(jnp.logical_not(root))
     def _():
-        gather_sent(pc, me_row, height, in_plane, plane_sems, pc_sems, skip=0)
+        pair_sent(pc, me_row, height, in_plane, plane_sems, pc_sems, skip=0)
 
 
 def spread(own, height, breadth):
@@ -359,8 +408,7 @@
             (lax.rem(me_row + 1, height), me_col),
         ).wait_recv()
 
-    gather_axis(wc, me_row, height, in_plane, plane_sems, wc_sems)
-    gather_received(wc, me_row, height, in_plane, plane_sems, wc_sems)
+    pair_gather(wc, me_row, height, in_plane, plane_sems, wc_sems)
     partial = jnp.zeros((B, B), f32)
     for i in range(height):
         partial = partial + product_nt(wc[i], vc[:, i * width : (i + 1) * width])
@@ -380,7 +428,7 @@
         role.wait_send()
 
     gather_sent(wr, me_col, breadth, in_line, line_sems, wr_sems)
-    gather_sent(wc, me_row, height, in_plane, plane_sems, wc_sems)
+    pair_sent(wc, me_row, height, in_plane, plane_sems, wc_sems)
     gather_sent(ex, me_col, breadth, in_line, ex_sends, ex_recvs)
 
 
@@ -457,7 +505,7 @@
 
 def final(matrix, left, right):
     rows, cols = matrix.shape
-    tile = min(256, rows)
+    tile = min(512, rows)
     depth = left.shape[1]
     return pl.pallas_call(
         final_kernel,

time: 155 us -> 145 us (0.935)
  Pallas kernels: 152 us -> 143 us
    pallas_call x1, Pallas kernels: 50.2 us -> 45.3 us  [images(): pl.pallas_call(lambda *refs: image_kernel(height, breadth, *refs), out_sh...]
    pallas_call x1, Pallas kernels: 27 us -> 24.5 us  [final(): pl.pallas_call(final_kernel, grid=(rows // tile,), out_shape=jax.ShapeDty...]
    pallas_call x1, Pallas kernels: 36.6 us -> 34.4 us  [spread(): pl.pallas_call(lambda *refs: spread_kernel(height, breadth, *refs), out_s...]
where the time goes in v4:
time: 145 us
  Pallas kernels  143 us (99%)
    pallas_call x1, Pallas kernels, images(): pl.pallas_call(lambda *refs: image_kernel(height, breadth, *refs), out_sh...  45.3 us
    pallas_call x1, Pallas kernels, spread(): pl.pallas_call(lambda *refs: spread_kernel(height, breadth, *refs), out_s...  34.4 us
    pallas_call x1, Pallas kernels, final(): pl.pallas_call(final_kernel, grid=(rows // tile,), out_shape=jax.ShapeDty...  24.5 us
    pallas_call x1, Pallas kernels, vectors_of(): pl.pallas_call(lambda *refs: vectors_kernel(height, breadth, *refs), out_...  17.6 us
    pallas_call x1, Pallas kernels, image_part(): pl.pallas_call(image_part_kernel, grid=(rows // width,), out_shape=jax.Sh...  15.3 us
    pallas_call x1, Pallas kernels, updates(): pl.pallas_call(lambda *refs: updates_kernel(height, breadth, *refs), out_...  5.54 us

profile of v4, /device:TPU:0, one launch (start us, length us, event | category | flops | bytes accessed | tf_op | source)
XLA Modules:
  0.0 145.0 jit_solution(10750623498559632982)
XLA Ops:
  0.0 1.3 slice_select_fusion
  1.3 1.1 copy.5
  2.4 34.4 %spread.1 = (f32[8,64,512]{2,1,0:T(8,128)}, f32[4,64,512]{2,1,0:T(8,128)}, f32[64,128]{1,0:T(8,128)}) custom-call(f32[8,64,512]{2,1,0:T(8,128)} %bitcast.7), custom_call_target="tpu_custom_call" | custom-call | tf_op jit(solution)/shard_map/spread/pallas_call | solution.py:296
  36.8 17.6 %vectors.1 = (f32[64,4096]{1,0:T(8,128)}, f32[64,2048]{1,0:T(8,128)}, f32[64,64]{1,0:T(8,128)}, f32[64,64]{1,0:T(8,128)}, bf16[128,4096]{1,0:T(8,128)(2,1)}) custom-call(f32[64,128]{1,0:T(8,128)} %get-tuple-element.18.refs_0_, f32[8,64,512]{2,1,0:T(8,128)} %get-tuple-element.19.refs_1_, f32[4,64,512]{2,1,0:T(8,128)} %get-tuple-element.20.refs_2_), custom_call_target="tpu_custom_call" | custom-call | tf_op jit(solution)/shard_map/vectors/pallas_call | solution.py:348
  54.4 15.3 %image_part.1.refs_0_ = f32[4,64,512]{2,1,0:T(8,128)} custom-call(f32[2048,4096]{1,0:T(8,128)} %block.3, bf16[128,4096]{1,0:T(8,128)(2,1)} %get-tuple-element.21.halves), custom_call_target="tpu_custom_call" | custom-call | tf_op jit(solution)/shard_map/image_part/pallas_call | solution.py:483
  69.7 45.3 %images.1 = (f32[8,64,512]{2,1,0:T(8,128)}, f32[4,64,512]{2,1,0:T(8,128)}, f32[64,128]{1,0:T(8,128)}) custom-call(f32[4,64,512]{2,1,0:T(8,128)} %image_part.1.refs_0_, f32[64,4096]{1,0:T(8,128)} %get-tuple-element.22.refs_1_.refs_3_), custom_call_target="tpu_custom_call" | custom-call | tf_op jit(solution)/shard_map/images/pallas_call | solution.py:439
  115.0 5.5 %updates.1 = (bf16[2048,384]{1,0:T(8,128)(2,1)}, bf16[384,4096]{1,0:T(8,128)(2,1)}) custom-call(f32[64,128]{1,0:T(8,128)} %get-tuple-element.23.refs_0_, f32[64,64]{1,0:T(8,128)} %get-tuple-element.24.refs_1_, f32[64,64]{1,0:T(8,128)} %get-tuple-element.25.refs_2_, f32[64,4096]{1,0:T(8,128)} %get-tuple-element.22.refs_1_.refs_3_, ...), custom_call_target="tpu_custom_call" | custom-call | tf_op jit(solution)/shard_map/updates/pallas_call | solution.py:549
  120.5 24.5 %final.1 = f32[2048,4096]{1,0:T(8,128)} custom-call(f32[2048,4096]{1,0:T(8,128)} %block.3, bf16[2048,384]{1,0:T(8,128)(2,1)} %get-tuple-element.29.left, bf16[384,4096]{1,0:T(8,128)(2,1)} %get-tuple-element.30.right), custom_call_target="tpu_custom_call" | custom-call | tf_op jit(solution)/shard_map/final/pallas_call | solution.py:510
  (1 shorter events, 0.0 us)
